TPU v7x, 512 devices: a whole 4x8x8 slice. The times are simulated.
512 devices in a mesh: panel: 2 (over y_lo), lon: 16 (over z, core), lat: 16 (over y_hi, x).
Axes of the slice: x: 4, y: 8 (y_hi: 4, y_lo: 2; y = y_hi * 2 + y_lo), z: 8, core: 2. Of those that a mesh axis runs over, the one named last changes fastest.
Arguments:
- pressure: float32 [2, 256, 512, 128], P('panel', 'lat', 'lon'), may hold values from -6 to 6
- porosity: float32 [2, 256, 512, 128], P('panel', 'lat', 'lon'), may hold values from 0.5 to 2
- source: float32 [2, 256, 512, 128], P('panel', 'lat', 'lon'), may hold values from -6 to 6
- bulk: float32 [2, 256, 512, 128], P('panel', 'lat', 'lon'), may hold values from 0.5 to 2
- lat_codes: int32 [2, 2, 2, 512], P('panel', None, None, 'lon'), may hold values from 0 to 8158, as said below
- lat_weights: float32 [2, 4, 2, 2, 512], P('panel', None, None, None, 'lon'), may hold values from 0 to 1, as said below
- lon_codes: int32 [2, 2, 2, 256], P('panel', None, None, 'lat'), may hold values from 0 to 8174, as said below
- lon_weights: float32 [2, 4, 2, 2, 256], P('panel', None, None, None, 'lat'), may hold values from 0 to 1, as said below
Outputs:
- pressure_out: float32 [2, 256, 512, 128], P('panel', 'lat', 'lon')
- porosity_out: float32 [2, 256, 512, 128], P('panel', 'lat', 'lon')
Inputs may be any that keep to these rules, and one draw needn't show every extreme that they name: `lat_codes`: an intersection map of the shell, which may differ from draw to draw: code = a * 32 + c with a < 255 a latitude of the whole panel and c < 31 an offset inside the longitude block of the ghost cell. `lon_codes`: an intersection map of the shell, which may differ from draw to draw: code = b * 16 + r with b < 511 a longitude of the whole panel and r < 15 an offset inside the latitude block of the ghost cell. `lat_weights`: the four weights of a ghost cell are non-negative and sum to one. `lon_weights`: the four weights of a ghost cell are non-negative and sum to one.
All inputs are finite; a program needn't handle non-finite values.
Results may differ from a plain program's by a relative error of at most 0.0003.
Values sent between devices are 32-bit elements; how exact they have to be, the bound alone decides.
A program may use at most 64 MiB of HBM per device.

v0:
```python
import jax
import jax.numpy as jnp
from jax import lax
from jax.sharding import PartitionSpec as P

SWEEPS = 3
stencil_offsets = ((0, 0), (0, 1), (1, 0), (1, 1))
radial_weight = 0.25
buoyancy = 0.5
time_step = 0.04


def padded_2(cells, sides, width):
    for axis, dim in sides:
        count = lax.axis_size(axis)
        ends = count - 1
        head = lax.slice_in_dim(cells, 0, width, axis=dim)
        tail = lax.slice_in_dim(cells, cells.shape[dim] - width, cells.shape[dim], axis=dim)
        cells = jnp.concatenate(
            [
                lax.ppermute(tail, axis, [(i, (i + 1) % count) for i in range(ends)]),
                cells,
                lax.ppermute(head, axis, [((i + 1) % count, i) for i in range(ends)]),
            ],
            axis=dim,
        )
    return cells


def swapped(block, axis, distance):
    count = lax.axis_size(axis)
    route = []
    for low in range(count):
        high = low | 1 << distance
        if high != low and high < count:
            route += [(low, high), (high, low)]
    return lax.ppermute(block, axis, route)


def pad_last(values, before, after):
    widths = [(0, 0)] * (values.ndim - 1) + [(before, after)]
    return jnp.pad(values, widths)


def rim_terms(field, lat_codes, lat_weights, lon_codes, lon_weights, width):
    rows_dev, cols_dev, levels = field.shape
    first_row = lax.axis_index("lat") * rows_dev
    first_col = lax.axis_index("lon") * cols_dev
    chosen = lat_codes[:, :width]
    rows_at = chosen // cols_dev - first_row
    cols_at = chosen % cols_dev
    lat_total = jnp.zeros(chosen.shape + (levels,), jnp.float32)
    for corner, (row_step, col_step) in enumerate(stencil_offsets):
        target = rows_at + row_step
        inside = (target >= 0) & (target < rows_dev)
        picked = field[jnp.clip(target, 0, rows_dev - 1), cols_at + col_step]
        lat_total = (
            lat_total + jnp.where(inside, lat_weights[corner, :, :width], 0.0)[..., None] * picked
        )
    chosen = lon_codes[:, :width]
    cols_at = chosen // rows_dev - first_col
    rows_at = chosen % rows_dev
    lon_total = jnp.zeros(chosen.shape + (levels,), jnp.float32)
    for corner, (row_step, col_step) in enumerate(stencil_offsets):
        target = cols_at + col_step
        inside = (target >= 0) & (target < cols_dev)
        picked = field[rows_at + row_step, jnp.clip(target, 0, cols_dev - 1)]
        lon_total = (
            lon_total + jnp.where(inside, lon_weights[corner, :, :width], 0.0)[..., None] * picked
        )
    return (lat_total, lon_total)


def surround(field, width, lat_codes, lat_weights, lon_codes, lon_weights):
    rows_dev, cols_dev, levels = field.shape
    padded = padded_2(field, (("lat", 0), ("lon", 1)), width)
    lat_terms, lon_terms = rim_terms(field, lat_codes, lat_weights, lon_codes, lon_weights, width)
    lat_summed = lax.psum(lat_terms, "lat")
    lon_summed = lax.psum(lon_terms, "lon")
    arrived = swapped(jnp.concatenate([lat_summed, lon_summed], axis=2), "panel", 0)
    lat_rim = arrived[:, :, :cols_dev]
    lon_rim = arrived[:, :, cols_dev:]
    lat_index = lax.axis_index("lat")
    lon_index = lax.axis_index("lon")
    last_lat = lax.axis_size("lat") - 1
    last_lon = lax.axis_size("lon") - 1
    north = jnp.where(lat_index == 0, lat_rim[0][::-1], padded[:width, width : width + cols_dev])
    padded = padded.at[:width, width : width + cols_dev].set(north)
    south = jnp.where(
        lat_index == last_lat, lat_rim[1], padded[width + rows_dev :, width : width + cols_dev]
    )
    padded = padded.at[width + rows_dev :, width : width + cols_dev].set(south)
    west = jnp.where(
        lon_index == 0,
        jnp.moveaxis(lon_rim[0][::-1], 0, 1),
        padded[width : width + rows_dev, :width],
    )
    padded = padded.at[width : width + rows_dev, :width].set(west)
    east = jnp.where(
        lon_index == last_lon,
        jnp.moveaxis(lon_rim[1], 0, 1),
        padded[width : width + rows_dev, width + cols_dev :],
    )
    padded = padded.at[width : width + rows_dev, width + cols_dev :].set(east)
    return padded


def face_terms(mobility):
    lat_face = 0.5 * (mobility[..., :-1, 1:-1, :] + mobility[..., 1:, 1:-1, :])
    lon_face = 0.5 * (mobility[..., 1:-1, :-1, :] + mobility[..., 1:-1, 1:, :])
    inner = mobility[..., 1:-1, 1:-1, :]
    mean_rad = 0.5 * (inner[..., :-1] + inner[..., 1:])
    return (lat_face, lon_face, mean_rad)


def diagonal_sum(bulk, lat_face, lon_face, mean_rad):
    rad_face = radial_weight * mean_rad
    total = bulk + lat_face[..., :-1, :, :] + lat_face[..., 1:, :, :]
    total = total + lon_face[..., :, :-1, :] + lon_face[..., :, 1:, :]
    return total + pad_last(rad_face, 1, 0) + pad_last(rad_face, 0, 1)


def neighbour_total(padded, source, lat_face, lon_face, mean_rad):
    inner = padded[..., 1:-1, 1:-1, :]
    rad_face = radial_weight * mean_rad
    total = source + lat_face[..., :-1, :, :] * padded[..., :-2, 1:-1, :]
    total = total + lat_face[..., 1:, :, :] * padded[..., 2:, 1:-1, :]
    total = total + lon_face[..., :, :-1, :] * padded[..., 1:-1, :-2, :]
    total = total + lon_face[..., :, 1:, :] * padded[..., 1:-1, 2:, :]
    total = (
        total
        + pad_last(rad_face * inner[..., :-1], 1, 0)
        + pad_last(rad_face * inner[..., 1:], 0, 1)
    )
    return total


def advect(pressure_pad, porosity_pad, lat_face, lon_face, mean_rad, bulk):
    pressure_in = pressure_pad[..., 1:-1, 1:-1, :]
    porosity_in = porosity_pad[..., 2:-2, 2:-2, :]
    lat_speed = -lat_face * (pressure_pad[..., 1:, 1:-1, :] - pressure_pad[..., :-1, 1:-1, :])
    lat_left = 1.5 * porosity_pad[..., 1:-2, 2:-2, :] - 0.5 * porosity_pad[..., :-3, 2:-2, :]
    lat_right = 1.5 * porosity_pad[..., 2:-1, 2:-2, :] - 0.5 * porosity_pad[..., 3:, 2:-2, :]
    lat_flux = lat_speed * jnp.where(lat_speed > 0, lat_left, lat_right)
    lon_speed = -lon_face * (pressure_pad[..., 1:-1, 1:, :] - pressure_pad[..., 1:-1, :-1, :])
    lon_left = 1.5 * porosity_pad[..., 2:-2, 1:-2, :] - 0.5 * porosity_pad[..., 2:-2, :-3, :]
    lon_right = 1.5 * porosity_pad[..., 2:-2, 2:-1, :] - 0.5 * porosity_pad[..., 2:-2, 3:, :]
    lon_flux = lon_speed * jnp.where(lon_speed > 0, lon_left, lon_right)
    rad_speed = (
        -radial_weight * mean_rad * (pressure_in[..., 1:] - pressure_in[..., :-1])
        + buoyancy * mean_rad
    )
    rad_flux = rad_speed * jnp.where(rad_speed > 0, porosity_in[..., :-1], porosity_in[..., 1:])
    divergence = lat_flux[..., 1:, :, :] - lat_flux[..., :-1, :, :]
    divergence = divergence + lon_flux[..., :, 1:, :] - lon_flux[..., :, :-1, :]
    divergence = divergence + pad_last(rad_flux, 0, 1) - pad_last(rad_flux, 1, 0)
    return porosity_in - time_step * (divergence + bulk * pressure_in)


def body(pressure, porosity, source, bulk, lat_codes, lat_weights, lon_codes, lon_weights):
    current = pressure[0]
    porosity_now = porosity[0]
    source_now = source[0]
    bulk_now = bulk[0]
    lat_code_now = lat_codes[0]
    lat_weight_now = lat_weights[0]
    lon_code_now = lon_codes[0]
    lon_weight_now = lon_weights[0]
    levels = porosity_now.shape[-1]
    both_pad = surround(
        jnp.concatenate([porosity_now, current], axis=-1),
        2,
        lat_code_now,
        lat_weight_now,
        lon_code_now,
        lon_weight_now,
    )
    porosity_pad = both_pad[..., :levels]
    first_pad = both_pad[1:-1, 1:-1, levels:]
    near = porosity_pad[1:-1, 1:-1, :]
    mobility = near * near * near
    lat_face, lon_face, mean_rad = face_terms(mobility)
    denominator = diagonal_sum(bulk_now, lat_face, lon_face, mean_rad)
    for sweep_index in range(SWEEPS):
        if sweep_index == 0:
            padded = first_pad
        else:
            padded = surround(
                current, 1, lat_code_now, lat_weight_now, lon_code_now, lon_weight_now
            )
        current = neighbour_total(padded, source_now, lat_face, lon_face, mean_rad) / denominator
    pressure_pad = surround(current, 1, lat_code_now, lat_weight_now, lon_code_now, lon_weight_now)
    porosity_new = advect(pressure_pad, porosity_pad, lat_face, lon_face, mean_rad, bulk_now)
    return (current[None], porosity_new[None])


def solution(mesh):
    placed = (
        P("panel", "lat", "lon", None),
        P("panel", "lat", "lon", None),
        P("panel", "lat", "lon", None),
        P("panel", "lat", "lon", None),
        P("panel", None, None, "lon"),
        P("panel", None, None, None, "lon"),
        P("panel", None, None, "lat"),
        P("panel", None, None, None, "lat"),
    )
    return jax.shard_map(
        body,
        mesh=mesh,
        in_specs=placed,
        out_specs=(P("panel", "lat", "lon", None), P("panel", "lat", "lon", None)),
        check_vma=False,
    )
```

profile of v0, /device:TPU:296, one launch (start us, length us, event | category | flops | bytes accessed | tf_op | source)
XLA Modules:
  0.0 794.1 jit_solution(9546006194397543275)
XLA Ops:
  7.2 1.3 copy_bitcast_fusion
  8.6 3.4 collective-permute-start
  12.0 6.7 collective-permute-start.1
  20.1 0.9 gather_fusion.7
  21.0 0.9 gather_fusion.6
  21.9 0.9 gather_fusion.5
  22.9 0.9 gather_fusion.4
  25.6 1.3 gather_fusion.3
  26.9 1.3 gather_fusion.2
  28.2 1.3 gather_fusion.1
  29.5 1.3 gather_fusion
  30.7 0.8 multiply_add_fusion
  33.9 1.9 collective-permute-start.2
  35.9 4.9 collective-permute-start.3
  40.7 85.8 %all-reduce.15.cloned.1.call-done = f32[2,2,16,256]{3,2,1,0:T(8,128)} async-done(((f32[2,2,16,256]{3,2,1,0:T(8,128)}), f32[2,2,16,256]{3,2,1,0:T(8,128)}) %all-reduce.15.cloned.1.call-update) | async-done | bytes 65552 | tf_op jit(solution)/shard_map/psum | solution.py:79
  126.6 174.8 %all-reduce.13.cloned.1.call-done = f32[2,2,32,256]{3,2,1,0:T(8,128)} async-done(((f32[2,2,32,256]{3,2,1,0:T(8,128)}), f32[2,2,32,256]{3,2,1,0:T(8,128)}) %all-reduce.13.cloned.1.call-update) | async-done | bytes 131088 | tf_op jit(solution)/shard_map/psum | solution.py:78
  301.3 1.0 pad_maximum_fusion.5
  302.3 3.4 collective-permute-start.4
  307.0 2.8 collective-permute-done.4
  310.2 1.9 dynamic-slice_select_fusion
  312.1 1.7 scatter.54
  314.9 0.8 copy-done
  316.4 6.1 collective-permute-start.6
  325.3 1.9 collective-permute-start.5
  327.3 0.9 gather_fusion.11
  328.1 0.9 gather_fusion.10
  329.0 0.9 gather_fusion.9
  329.9 0.9 gather_fusion.8
  330.9 82.9 %psum.58 = f32[2,1,32,128]{3,2,1,0:T(8,128)S(1)} all-reduce(f32[2,1,32,128]{3,2,1,0:T(8,128)S(1)} %multiply_add_fusion.4), channel_id=1, replica_groups=mesh['panel'=2,'lon'=16,'lat'=16] {'lat'}, use_global_device_ids=true, to_apply=%region_3.4 | all-reduce | flops 8192 | bytes 65536 | tf_op jit(solution)/shard_map/psum | solution.py:78
  413.9 45.7 %psum.59 = f32[2,1,16,128]{3,2,1,0:T(8,128)S(1)} all-reduce(f32[2,1,16,128]{3,2,1,0:T(8,128)S(1)} %multiply_add_fusion.7), channel_id=1, replica_groups=mesh['panel'=2,'lon'=16,'lat'=16] {'lon'}, use_global_device_ids=true, to_apply=%region_4.5 | all-reduce | flops 4096 | bytes 32768 | tf_op jit(solution)/shard_map/psum | solution.py:79
  459.6 2.1 collective-permute-start.7
  461.8 4.9 collective-permute-start.8
  466.6 2.4 collective-permute-start.9
  469.2 3.5 collective-permute-done.9
  472.6 1.4 scatter.60
  474.7 0.8 copy-done.2
  479.0 0.9 gather_fusion.19
  479.9 0.9 gather_fusion.18
  480.8 0.9 gather_fusion.17
  481.7 0.9 gather_fusion.16
  482.5 1.9 collective-permute-start.11
  484.5 3.9 collective-permute-start.10
  488.5 80.9 %psum.60 = f32[2,1,32,128]{3,2,1,0:T(8,128)S(1)} all-reduce(f32[2,1,32,128]{3,2,1,0:T(8,128)S(1)} %multiply_add_fusion.3), channel_id=1, replica_groups=mesh['panel'=2,'lon'=16,'lat'=16] {'lat'}, use_global_device_ids=true, to_apply=%region_5.6 | all-reduce | flops 8192 | bytes 65536 | tf_op jit(solution)/shard_map/psum | solution.py:78
  569.5 45.7 %psum.61 = f32[2,1,16,128]{3,2,1,0:T(8,128)S(1)} all-reduce(f32[2,1,16,128]{3,2,1,0:T(8,128)S(1)} %multiply_add_fusion.6), channel_id=1, replica_groups=mesh['panel'=2,'lon'=16,'lat'=16] {'lon'}, use_global_device_ids=true, to_apply=%region_6.7 | all-reduce | flops 4096 | bytes 32768 | tf_op jit(solution)/shard_map/psum | solution.py:79
  615.2 1.9 collective-permute-start.12
  617.2 4.9 collective-permute-start.13
  622.0 2.4 collective-permute-start.14
  624.6 3.5 collective-permute-done.14
  628.0 1.4 scatter.66
  630.1 0.8 copy-done.3
  634.4 0.9 gather_fusion.27
  635.3 0.9 gather_fusion.26
  636.2 0.9 gather_fusion.25
  637.1 0.9 gather_fusion.24
  638.0 1.9 collective-permute-start.16
  639.9 3.9 collective-permute-start.15
  643.9 80.9 %psum.62 = f32[2,1,32,128]{3,2,1,0:T(8,128)S(1)} all-reduce(f32[2,1,32,128]{3,2,1,0:T(8,128)S(1)} %multiply_add_fusion.2), channel_id=1, replica_groups=mesh['panel'=2,'lon'=16,'lat'=16] {'lat'}, use_global_device_ids=true, to_apply=%region_7.8 | all-reduce | flops 8192 | bytes 65536 | tf_op jit(solution)/shard_map/psum | solution.py:78
  724.9 45.7 %psum.63 = f32[2,1,16,128]{3,2,1,0:T(8,128)S(1)} all-reduce(f32[2,1,16,128]{3,2,1,0:T(8,128)S(1)} %multiply_add_fusion.5), channel_id=1, replica_groups=mesh['panel'=2,'lon'=16,'lat'=16] {'lon'}, use_global_device_ids=true, to_apply=%region_8.9 | all-reduce | flops 4096 | bytes 32768 | tf_op jit(solution)/shard_map/psum | solution.py:79
  770.7 1.9 collective-permute-start.17
  772.6 4.9 collective-permute-start.18
  777.5 2.4 collective-permute-start.19
  779.9 0.8 copy.275
  780.8 2.7 collective-permute-done.19
  783.4 1.4 scatter.74
  (178 shorter events, 23.1 us)
Async XLA Ops:
  7.2 119.4 %all-reduce.15.cloned.1.call-start = ((), (), s32[]{:S(2)}) async-start(), calls=%async_computation.1 | async-start | bytes 131072 | tf_op jit(solution)/shard_map/psum | solution.py:79
  8.6 25.3 %collective-permute-start = (f32[2,32,256]{2,0,1:T(2,128)S(1)}, f32[2,32,256]{2,0,1:T(2,128)S(1)}, u32[]{:S(2)}, u32[]{:S(2)}) collective-permute-start(f32[2,32,256]{2,0,1:T(2,128)S(1)} %get-tuple-element.224), channel_id=1, source_target_pairs={{0,1},{1,2},{2,3},{3,4},{4,5},{5,6},{6,7},{7,8},{8,9},{9,10},{10,1... | collective-permute-start | bytes 196616 | tf_op jit(solution)/shard_map/ppermute | solution.py:21
  12.0 21.9 %collective-permute-start.1 = (f32[2,32,256]{2,0,1:T(2,128)S(1)}, f32[2,32,256]{2,0,1:T(2,128)S(1)}, u32[]{:S(2)}, u32[]{:S(2)}) collective-permute-start(f32[2,32,256]{2,0,1:T(2,128)S(1)} %get-tuple-element.225), channel_id=1, source_target_pairs={{1,0},{2,1},{3,2},{4,3},{5,4},{6,5},{7,6},{8,7},{9,8},{10,9},{11,1... | collective-permute-start | bytes 196616 | tf_op jit(solution)/shard_map/ppermute | solution.py:23
  18.7 0.7 copy-start.6
  18.7 0.7 copy-start.4
  24.5 0.7 copy-start.7
  24.5 0.7 copy-start.5
  24.5 276.8 %all-reduce.13.cloned.1.call-start = ((), (), s32[]{:S(2)}) async-start(), calls=%async_computation | async-start | bytes 262144 | tf_op jit(solution)/shard_map/psum | solution.py:78
  31.9 0.7 copy-start.8
  33.9 273.0 %collective-permute-start.2 = (f32[20,2,256]{2,0,1:T(8,128)S(1)}, f32[20,2,256]{2,0,1:T(8,128)S(1)}, u32[]{:S(2)}, u32[]{:S(2)}) collective-permute-start(f32[20,2,256]{2,0,1:T(8,128)S(1)} %get-tuple-element.222), channel_id=1, source_target_pairs={{0,16},{16,32},{32,48},{48,64},{64,80},{80,96},{96,112},{112,128},... | collective-permute-start | bytes 122888 | tf_op jit(solution)/shard_map/ppermute | solution.py:21
  35.9 271.0 %collective-permute-start.3 = (f32[20,2,256]{2,0,1:T(8,128)S(1)}, f32[20,2,256]{2,0,1:T(8,128)S(1)}, u32[]{:S(2)}, u32[]{:S(2)}) collective-permute-start(f32[20,2,256]{2,0,1:T(8,128)S(1)} %get-tuple-element.223), channel_id=1, source_target_pairs={{16,0},{32,16},{48,32},{64,48},{80,64},{96,80},{112,96},{128,112},... | collective-permute-start | bytes 122888 | tf_op jit(solution)/shard_map/ppermute | solution.py:23
  302.3 7.6 collective-permute-start.4
  314.7 1.0 copy-start
  314.7 1.0 copy-start.1
  316.4 143.2 %collective-permute-start.6 = (f32[1,32,128]{2,0,1:T(1,128)S(1)}, f32[1,32,128]{2,0,1:T(1,128)S(1)}, u32[]{:S(2)}, u32[]{:S(2)}) collective-permute-start(f32[1,32,128]{2,0,1:T(1,128)S(1)} %slice.1083), channel_id=1, source_target_pairs={{1,0},{2,1},{3,2},{4,3},{5,4},{6,5},{7,6},{8,7},{9,8},{10,9},{11,1... | collective-permute-start | bytes 49160 | tf_op jit(solution)/shard_map/ppermute | solution.py:23
  325.3 134.3 %collective-permute-start.5 = (f32[1,32,128]{2,1,0:T(8,128)S(1)}, f32[1,32,128]{2,1,0:T(8,128)S(1)}, u32[]{:S(2)}, u32[]{:S(2)}) collective-permute-start(f32[1,32,128]{2,1,0:T(8,128)S(1)} %slice.1082), channel_id=1, source_target_pairs={{0,1},{1,2},{2,3},{3,4},{4,5},{5,6},{6,7},{7,8},{8,9},{9,10},{10,1... | collective-permute-start | bytes 49160 | tf_op jit(solution)/shard_map/ppermute | solution.py:21
  459.6 9.4 %collective-permute-start.7 = (f32[18,1,128]{2,0,1:T(8,128)S(1)}, f32[18,1,128]{2,0,1:T(8,128)S(1)}, u32[]{:S(2)}, u32[]{:S(2)}) collective-permute-start(f32[18,1,128]{2,0,1:T(8,128)S(1)} %get-tuple-element.230), channel_id=1, source_target_pairs={{0,16},{16,32},{32,48},{48,64},{64,80},{80,96},{96,112},{112,128},... | collective-permute-start | bytes 27656 | tf_op jit(solution)/shard_map/ppermute | solution.py:21
  461.8 7.3 collective-permute-start.8
  466.6 6.0 collective-permute-start.9
  474.6 1.0 copy-start.2
  482.5 132.7 %collective-permute-start.11 = (f32[1,32,128]{2,0,1:T(1,128)S(1)}, f32[1,32,128]{2,0,1:T(1,128)S(1)}, u32[]{:S(2)}, u32[]{:S(2)}) collective-permute-start(f32[1,32,128]{2,0,1:T(1,128)S(1)} %slice.1124), channel_id=1, source_target_pairs={{1,0},{2,1},{3,2},{4,3},{5,4},{6,5},{7,6},{8,7},{9,8},{10,9},{11,1... | collective-permute-start | bytes 49160 | tf_op jit(solution)/shard_map/ppermute | solution.py:23
  484.5 130.7 %collective-permute-start.10 = (f32[1,32,128]{2,1,0:T(8,128)S(1)}, f32[1,32,128]{2,1,0:T(8,128)S(1)}, u32[]{:S(2)}, u32[]{:S(2)}) collective-permute-start(f32[1,32,128]{2,1,0:T(8,128)S(1)} %slice.1123), channel_id=1, source_target_pairs={{0,1},{1,2},{2,3},{3,4},{4,5},{5,6},{6,7},{7,8},{8,9},{9,10},{10,1... | collective-permute-start | bytes 49160 | tf_op jit(solution)/shard_map/ppermute | solution.py:21
  615.2 9.2 %collective-permute-start.12 = (f32[18,1,128]{2,0,1:T(8,128)S(1)}, f32[18,1,128]{2,0,1:T(8,128)S(1)}, u32[]{:S(2)}, u32[]{:S(2)}) collective-permute-start(f32[18,1,128]{2,0,1:T(8,128)S(1)} %get-tuple-element.228), channel_id=1, source_target_pairs={{0,16},{16,32},{32,48},{48,64},{64,80},{80,96},{96,112},{112,128},... | collective-permute-start | bytes 27656 | tf_op jit(solution)/shard_map/ppermute | solution.py:21
  617.2 7.3 collective-permute-start.13
  622.0 6.0 collective-permute-start.14
  630.0 1.0 copy-start.3
  638.0 132.7 %collective-permute-start.16 = (f32[1,32,128]{2,0,1:T(1,128)S(1)}, f32[1,32,128]{2,0,1:T(1,128)S(1)}, u32[]{:S(2)}, u32[]{:S(2)}) collective-permute-start(f32[1,32,128]{2,0,1:T(1,128)S(1)} %slice.1140), channel_id=1, source_target_pairs={{1,0},{2,1},{3,2},{4,3},{5,4},{6,5},{7,6},{8,7},{9,8},{10,9},{11,1... | collective-permute-start | bytes 49160 | tf_op jit(solution)/shard_map/ppermute | solution.py:23
  639.9 130.7 %collective-permute-start.15 = (f32[1,32,128]{2,1,0:T(8,128)S(1)}, f32[1,32,128]{2,1,0:T(8,128)S(1)}, u32[]{:S(2)}, u32[]{:S(2)}) collective-permute-start(f32[1,32,128]{2,1,0:T(8,128)S(1)} %slice.1139), channel_id=1, source_target_pairs={{0,1},{1,2},{2,3},{3,4},{4,5},{5,6},{6,7},{7,8},{8,9},{9,10},{10,1... | collective-permute-start | bytes 49160 | tf_op jit(solution)/shard_map/ppermute | solution.py:21
  770.7 10.0 %collective-permute-start.17 = (f32[18,1,128]{2,0,1:T(8,128)S(1)}, f32[18,1,128]{2,0,1:T(8,128)S(1)}, u32[]{:S(2)}, u32[]{:S(2)}) collective-permute-start(f32[18,1,128]{2,0,1:T(8,128)S(1)} %get-tuple-element.226), channel_id=1, source_target_pairs={{0,16},{16,32},{32,48},{48,64},{64,80},{80,96},{96,112},{112,128},... | collective-permute-start | bytes 27656 | tf_op jit(solution)/shard_map/ppermute | solution.py:21
  772.6 8.1 %collective-permute-start.18 = (f32[18,1,128]{2,0,1:T(8,128)S(1)}, f32[18,1,128]{2,0,1:T(8,128)S(1)}, u32[]{:S(2)}, u32[]{:S(2)}) collective-permute-start(f32[18,1,128]{2,0,1:T(8,128)S(1)} %get-tuple-element.227), channel_id=1, source_target_pairs={{16,0},{32,16},{48,32},{64,48},{80,64},{96,80},{112,96},{128,112},... | collective-permute-start | bytes 27656 | tf_op jit(solution)/shard_map/ppermute | solution.py:23
  777.5 6.0 collective-permute-start.19
Sparse Core Ops, SparseCore 0:
  24.6 101.8 all-reduce.14
  130.0 171.2 all-reduce.12
where the time goes:
time: 795 us; the launch traced here: 794 us
  blocking collectives  382 us (48%)
  waiting for transfers between devices  273 us (34%)
  starting transfers between devices  67.7 us (9%)
  local copies, waits for them, and re-layouts  46.2 us (6%)
  between operations  15.1 us (2%)
  other arithmetic  10.1 us (1%)
    psum x3, blocking collectives, surround(): lat_summed = lax.psum(lat_terms, 'lat')  245 us
    psum x1, waiting for transfers between devices, surround(): lat_summed = lax.psum(lat_terms, 'lat')  175 us
    psum x3, blocking collectives, surround(): lon_summed = lax.psum(lon_terms, 'lon')  137 us
    psum x1, waiting for transfers between devices, surround(): lon_summed = lax.psum(lon_terms, 'lon')  85.8 us
    ppermute x8, starting transfers between devices, padded_2(): lax.ppermute(head, axis, [((i + 1) % count, i) for i in range(ends)])  36 us
    ppermute x8, starting transfers between devices, padded_2(): lax.ppermute(tail, axis, [(i, (i + 1) % count) for i in range(ends)])  21 us
  transfers between devices with their start and end apart: 22, of which 6 were waited for; matrix products, arithmetic and copies ran while one was open for 3% of the time, Pallas kernels for 0%

commit v1 on v0

--- a/solution.py
+++ b/solution.py
@@ -76,7 +76,11 @@
     padded = padded_2(field, (("lat", 0), ("lon", 1)), width)
     lat_terms, lon_terms = rim_terms(field, lat_codes, lat_weights, lon_codes, lon_weights, width)
     lat_summed = lax.psum(lat_terms, "lat")
-    lon_summed = lax.psum(lon_terms, "lon")
+    lon_summed = lon_terms
+    for hop in (1, 2, 4, 8):
+        lon_summed = lon_summed + lax.ppermute(
+            lon_summed, "lon", [(dev, dev ^ hop) for dev in range(16)]
+        )
     arrived = swapped(jnp.concatenate([lat_summed, lon_summed], axis=2), "panel", 0)
     lat_rim = arrived[:, :, :cols_dev]
     lon_rim = arrived[:, :, cols_dev:]

time: 795 us -> 608 us (0.76)
  the two profiles are of different devices: /device:TPU:296 before, /device:TPU:168 now
where the time goes in v1:
time: 608 us; the launch traced here: 606 us
  blocking collectives  245 us (40%)
  waiting for transfers between devices  170 us (28%)
  starting transfers between devices  122 us (20%)
  local copies, waits for them, and re-layouts  44.7 us (7%)
  between operations  15.5 us (3%)
  other arithmetic  9.69 us (2%)
    psum x3, blocking collectives, surround(): lat_summed = lax.psum(lat_terms, 'lat')  245 us
    psum x1, waiting for transfers between devices, surround(): lat_summed = lax.psum(lat_terms, 'lat')  141 us
    ppermute x16, starting transfers between devices, surround(): lax.ppermute(lon_summed, 'lon', [(dev, dev ^ hop) for dev in range(16)])  59.1 us
    ppermute x8, starting transfers between devices, padded_2(): lax.ppermute(head, axis, [((i + 1) % count, i) for i in range(ends)])  31.1 us
    ppermute x8, starting transfers between devices, padded_2(): lax.ppermute(tail, axis, [(i, (i + 1) % count) for i in range(ends)])  20.8 us
    gather x16, local copies, waits for them, and re-layouts, rim_terms(): picked = field[jnp.clip(target, 0, rows_dev - 1), cols_at + col_step]  15.7 us
    ppermute x16, waiting for transfers between devices, surround(): lax.ppermute(lon_summed, 'lon', [(dev, dev ^ hop) for dev in range(16)])  14.8 us
    ppermute x4, waiting for transfers between devices, swapped(): return lax.ppermute(block, axis, route)  13.5 us
  transfers between devices with their start and end apart: 37, of which 10 were waited for; matrix products, arithmetic and copies ran while one was open for 4% of the time, Pallas kernels for 0%

profile of v1, /device:TPU:168, one launch (start us, length us, event | category | flops | bytes accessed | tf_op | source)
XLA Modules:
  0.0 606.2 jit_solution(17670497854500235593)
XLA Ops:
  7.2 1.3 copy_bitcast_fusion
  8.6 3.4 collective-permute-start
  12.0 6.7 %collective-permute-start.1 = (f32[2,32,256]{2,0,1:T(2,128)S(1)}, f32[2,32,256]{2,0,1:T(2,128)S(1)}, u32[]{:S(2)}, u32[]{:S(2)}) collective-permute-start(f32[2,32,256]{2,0,1:T(2,128)S(1)} %get-tuple-element.225), channel_id=1, source_target_pairs={{1,0},{2,1},{3,2},{4,3},{5,4},{6,5},{7,6},{8,7},{9,8},{10,9},{11,1... | collective-permute-start | bytes 196616 | tf_op jit(solution)/shard_map/ppermute | solution.py:23
  20.1 0.9 gather_fusion.7
  21.0 0.9 gather_fusion.6
  21.9 0.9 gather_fusion.5
  22.9 0.9 gather_fusion.4
  23.9 1.9 collective-permute-start.4
  26.3 1.3 gather_fusion.3
  27.5 1.3 gather_fusion.2
  28.8 1.3 gather_fusion.1
  30.1 1.3 gather_fusion
  32.6 4.3 collective-permute-start.5
  37.0 2.7 collective-permute-done.5
  39.7 1.9 collective-permute-start.6
  42.4 4.4 collective-permute-done.6
  46.8 8.6 %collective-permute-start.7 = (f32[2,2,16,256]{3,2,1,0:T(8,128)S(1)}, f32[2,2,16,256]{3,2,1,0:T(8,128)S(1)}, u32[]{:S(2)}, u32[]{:S(2)}) collective-permute-start(f32[2,2,16,256]{3,2,1,0:T(8,128)S(1)} %add.807), channel_id=1, source_target_pairs={{0,128},{16,144},{32,160},{48,176},{64,192},{80,208},{96,224},{112... | collective-permute-start | bytes 196616 | tf_op jit(solution)/shard_map/ppermute | solution.py:81
  55.4 1.9 collective-permute-start.2
  57.3 3.6 collective-permute-start.3
  61.0 141.4 %all-reduce.12.cloned.1.call-done = f32[2,2,32,256]{3,2,1,0:T(8,128)} async-done(((f32[2,2,32,256]{3,2,1,0:T(8,128)}), f32[2,2,32,256]{3,2,1,0:T(8,128)}) %all-reduce.12.cloned.1.call-update) | async-done | bytes 131088 | tf_op jit(solution)/shard_map/psum | solution.py:78
  202.4 0.9 pad_maximum_fusion.5
  203.3 3.4 collective-permute-start.8
  207.8 3.2 collective-permute-done.8
  211.2 2.0 dynamic-slice_select_fusion
  213.2 1.7 scatter.54
  220.4 1.9 collective-permute-start.13
  223.3 6.1 %collective-permute-start.10 = (f32[1,32,128]{2,0,1:T(1,128)S(1)}, f32[1,32,128]{2,0,1:T(1,128)S(1)}, u32[]{:S(2)}, u32[]{:S(2)}) collective-permute-start(f32[1,32,128]{2,0,1:T(1,128)S(1)} %slice.1083), channel_id=1, source_target_pairs={{1,0},{2,1},{3,2},{4,3},{5,4},{6,5},{7,6},{8,7},{9,8},{10,9},{11,1... | collective-permute-start | bytes 49160 | tf_op jit(solution)/shard_map/ppermute | solution.py:23
  229.4 1.9 collective-permute-start.9
  234.9 3.6 collective-permute-start.14
  238.5 2.0 collective-permute-done.14
  240.5 2.1 collective-permute-start.15
  242.6 82.9 %psum.29 = f32[2,1,32,128]{3,2,1,0:T(8,128)S(1)} all-reduce(f32[2,1,32,128]{3,2,1,0:T(8,128)S(1)} %multiply_add_fusion.4), channel_id=1, replica_groups=mesh['panel'=2,'lon'=16,'lat'=16] {'lat'}, use_global_device_ids=true, to_apply=%region_2.3 | all-reduce | flops 8192 | bytes 65536 | tf_op jit(solution)/shard_map/psum | solution.py:78
  325.5 8.1 %collective-permute-start.16 = (f32[2,1,16,128]{3,2,1,0:T(8,128)S(1)}, f32[2,1,16,128]{3,2,1,0:T(8,128)S(1)}, u32[]{:S(2)}, u32[]{:S(2)}) collective-permute-start(f32[2,1,16,128]{3,2,1,0:T(8,128)S(1)} %add.848), channel_id=1, source_target_pairs={{0,128},{16,144},{32,160},{48,176},{64,192},{80,208},{96,224},{112... | collective-permute-start | bytes 49160 | tf_op jit(solution)/shard_map/ppermute | solution.py:81
  333.6 1.9 collective-permute-start.11
  335.5 3.6 collective-permute-start.12
  339.2 2.4 collective-permute-start.17
  341.8 3.5 collective-permute-done.17
  345.2 1.4 scatter.60
  351.6 1.9 collective-permute-start.22
  357.1 1.9 collective-permute-start.19
  359.0 3.9 collective-permute-start.18
  363.0 2.7 collective-permute-start.23
  365.7 2.9 collective-permute-done.23
  368.6 1.9 collective-permute-start.24
  370.5 80.9 %psum.30 = f32[2,1,32,128]{3,2,1,0:T(8,128)S(1)} all-reduce(f32[2,1,32,128]{3,2,1,0:T(8,128)S(1)} %multiply_add_fusion.3), channel_id=1, replica_groups=mesh['panel'=2,'lon'=16,'lat'=16] {'lat'}, use_global_device_ids=true, to_apply=%region_3.4 | all-reduce | flops 8192 | bytes 65536 | tf_op jit(solution)/shard_map/psum | solution.py:78
  451.5 5.6 collective-permute-start.25
  457.1 1.9 collective-permute-start.20
  459.1 3.6 collective-permute-start.21
  462.7 2.4 collective-permute-start.26
  465.3 3.5 collective-permute-done.26
  468.7 1.4 scatter.66
  475.1 1.9 collective-permute-start.31
  480.6 1.9 collective-permute-start.28
  482.5 3.9 collective-permute-start.27
  486.5 2.7 collective-permute-start.32
  489.3 2.8 collective-permute-done.32
  492.1 3.0 collective-permute-start.33
  495.2 80.9 %psum.31 = f32[2,1,32,128]{3,2,1,0:T(8,128)S(1)} all-reduce(f32[2,1,32,128]{3,2,1,0:T(8,128)S(1)} %multiply_add_fusion.2), channel_id=1, replica_groups=mesh['panel'=2,'lon'=16,'lat'=16] {'lat'}, use_global_device_ids=true, to_apply=%region_4.5 | all-reduce | flops 8192 | bytes 65536 | tf_op jit(solution)/shard_map/psum | solution.py:78
  576.8 7.1 %collective-permute-start.34 = (f32[2,1,16,128]{3,2,1,0:T(8,128)S(1)}, f32[2,1,16,128]{3,2,1,0:T(8,128)S(1)}, u32[]{:S(2)}, u32[]{:S(2)}) collective-permute-start(f32[2,1,16,128]{3,2,1,0:T(8,128)S(1)} %add.880), channel_id=1, source_target_pairs={{0,128},{16,144},{32,160},{48,176},{64,192},{80,208},{96,224},{112... | collective-permute-start | bytes 49160 | tf_op jit(solution)/shard_map/ppermute | solution.py:81
  584.0 1.9 collective-permute-start.29
  585.9 3.6 collective-permute-start.30
  589.6 2.4 collective-permute-start.35
  592.1 3.5 collective-permute-done.35
  595.6 1.4 scatter.74
  (220 shorter events, 35.8 us)
Async XLA Ops:
  7.2 195.3 %all-reduce.12.cloned.1.call-start = ((), (), s32[]{:S(2)}) async-start(), calls=%async_computation | async-start | bytes 262144 | tf_op jit(solution)/shard_map/psum | solution.py:78
  8.6 46.7 %collective-permute-start = (f32[2,32,256]{2,0,1:T(2,128)S(1)}, f32[2,32,256]{2,0,1:T(2,128)S(1)}, u32[]{:S(2)}, u32[]{:S(2)}) collective-permute-start(f32[2,32,256]{2,0,1:T(2,128)S(1)} %get-tuple-element.224), channel_id=1, source_target_pairs={{0,1},{1,2},{2,3},{3,4},{4,5},{5,6},{6,7},{7,8},{8,9},{9,10},{10,1... | collective-permute-start | bytes 196616 | tf_op jit(solution)/shard_map/ppermute | solution.py:21
  12.0 43.3 %collective-permute-start.1 = (f32[2,32,256]{2,0,1:T(2,128)S(1)}, f32[2,32,256]{2,0,1:T(2,128)S(1)}, u32[]{:S(2)}, u32[]{:S(2)}) collective-permute-start(f32[2,32,256]{2,0,1:T(2,128)S(1)} %get-tuple-element.225), channel_id=1, source_target_pairs={{1,0},{2,1},{3,2},{4,3},{5,4},{6,5},{7,6},{8,7},{9,8},{10,9},{11,1... | collective-permute-start | bytes 196616 | tf_op jit(solution)/shard_map/ppermute | solution.py:23
  18.7 0.7 copy-start.6
  18.7 0.7 copy-start.4
  23.8 2.1 copy-start.7
  23.9 2.0 copy-start.5
  23.9 8.7 %collective-permute-start.4 = (f32[2,2,16,256]{3,2,1,0:T(8,128)S(1)}, f32[2,2,16,256]{3,2,1,0:T(8,128)S(1)}, u32[]{:S(2)}, u32[]{:S(2)}) collective-permute-start(f32[2,2,16,256]{3,2,1,0:T(8,128)S(1)} %multiply_add_fusion.1), channel_id=1, source_target_pairs={{0,16},{16,0},{32,48},{48,32},{64,80},{80,64},{96,112},{112,96},{1... | collective-permute-start | bytes 196616 | tf_op jit(solution)/shard_map/ppermute | solution.py:81
  32.6 7.0 %collective-permute-start.5 = (f32[2,2,16,256]{3,2,1,0:T(8,128)S(1)}, f32[2,2,16,256]{3,2,1,0:T(8,128)S(1)}, u32[]{:S(2)}, u32[]{:S(2)}) collective-permute-start(f32[2,2,16,256]{3,2,1,0:T(8,128)S(1)} %add.805), channel_id=1, source_target_pairs={{0,32},{16,48},{32,0},{48,16},{64,96},{80,112},{96,64},{112,80},{1... | collective-permute-start | bytes 196616 | tf_op jit(solution)/shard_map/ppermute | solution.py:81
  36.9 4.7 copy-start.8
  39.7 7.1 %collective-permute-start.6 = (f32[2,2,16,256]{3,2,1,0:T(8,128)S(1)}, f32[2,2,16,256]{3,2,1,0:T(8,128)S(1)}, u32[]{:S(2)}, u32[]{:S(2)}) collective-permute-start(f32[2,2,16,256]{3,2,1,0:T(8,128)S(1)} %add.806), channel_id=1, source_target_pairs={{0,64},{16,80},{32,96},{48,112},{64,0},{80,16},{96,32},{112,48},{1... | collective-permute-start | bytes 196616 | tf_op jit(solution)/shard_map/ppermute | solution.py:81
  46.8 14.2 %collective-permute-start.7 = (f32[2,2,16,256]{3,2,1,0:T(8,128)S(1)}, f32[2,2,16,256]{3,2,1,0:T(8,128)S(1)}, u32[]{:S(2)}, u32[]{:S(2)}) collective-permute-start(f32[2,2,16,256]{3,2,1,0:T(8,128)S(1)} %add.807), channel_id=1, source_target_pairs={{0,128},{16,144},{32,160},{48,176},{64,192},{80,208},{96,224},{112... | collective-permute-start | bytes 196616 | tf_op jit(solution)/shard_map/ppermute | solution.py:81
  55.4 152.2 %collective-permute-start.2 = (f32[20,2,256]{2,0,1:T(8,128)S(1)}, f32[20,2,256]{2,0,1:T(8,128)S(1)}, u32[]{:S(2)}, u32[]{:S(2)}) collective-permute-start(f32[20,2,256]{2,0,1:T(8,128)S(1)} %get-tuple-element.222), channel_id=1, source_target_pairs={{0,16},{16,32},{32,48},{48,64},{64,80},{80,96},{96,112},{112,128},... | collective-permute-start | bytes 122888 | tf_op jit(solution)/shard_map/ppermute | solution.py:21
  57.3 150.3 %collective-permute-start.3 = (f32[20,2,256]{2,0,1:T(8,128)S(1)}, f32[20,2,256]{2,0,1:T(8,128)S(1)}, u32[]{:S(2)}, u32[]{:S(2)}) collective-permute-start(f32[20,2,256]{2,0,1:T(8,128)S(1)} %get-tuple-element.223), channel_id=1, source_target_pairs={{16,0},{32,16},{48,32},{64,48},{80,64},{96,80},{112,96},{128,112},... | collective-permute-start | bytes 122888 | tf_op jit(solution)/shard_map/ppermute | solution.py:23
  203.3 7.6 %collective-permute-start.8 = (f32[2,2,48,256]{3,2,1,0:T(8,128)S(1)}, f32[2,2,48,256]{3,2,1,0:T(8,128)S(1)}, u32[]{:S(2)}, u32[]{:S(2)}) collective-permute-start(f32[2,2,48,256]{3,2,1,0:T(8,128)S(1)} %pad_maximum_fusion.5), channel_id=1, source_target_pairs={{0,256},{256,0},{1,257},{257,1},{2,258},{258,2},{3,259},{259,3},{4... | collective-permute-start | bytes 589832 | tf_op jit(solution)/shard_map/ppermute | solution.py:37
  215.8 1.0 copy-start
  215.8 1.0 copy-start.1
  220.4 14.4 %collective-permute-start.13 = (f32[2,1,16,128]{3,2,1,0:T(8,128)S(1)}, f32[2,1,16,128]{3,2,1,0:T(8,128)S(1)}, u32[]{:S(2)}, u32[]{:S(2)}) collective-permute-start(f32[2,1,16,128]{3,2,1,0:T(8,128)S(1)} %multiply_add_fusion.7), channel_id=1, source_target_pairs={{0,16},{16,0},{32,48},{48,32},{64,80},{80,64},{96,112},{112,96},{1... | collective-permute-start | bytes 49160 | tf_op jit(solution)/shard_map/ppermute | solution.py:81
  223.3 110.3 %collective-permute-start.10 = (f32[1,32,128]{2,0,1:T(1,128)S(1)}, f32[1,32,128]{2,0,1:T(1,128)S(1)}, u32[]{:S(2)}, u32[]{:S(2)}) collective-permute-start(f32[1,32,128]{2,0,1:T(1,128)S(1)} %slice.1083), channel_id=1, source_target_pairs={{1,0},{2,1},{3,2},{4,3},{5,4},{6,5},{7,6},{8,7},{9,8},{10,9},{11,1... | collective-permute-start | bytes 49160 | tf_op jit(solution)/shard_map/ppermute | solution.py:23
  229.4 104.2 %collective-permute-start.9 = (f32[1,32,128]{2,1,0:T(8,128)S(1)}, f32[1,32,128]{2,1,0:T(8,128)S(1)}, u32[]{:S(2)}, u32[]{:S(2)}) collective-permute-start(f32[1,32,128]{2,1,0:T(8,128)S(1)} %slice.1082), channel_id=1, source_target_pairs={{0,1},{1,2},{2,3},{3,4},{4,5},{5,6},{6,7},{7,8},{8,9},{9,10},{10,1... | collective-permute-start | bytes 49160 | tf_op jit(solution)/shard_map/ppermute | solution.py:21
  234.9 5.6 collective-permute-start.14
  240.5 85.0 %collective-permute-start.15 = (f32[2,1,16,128]{3,2,1,0:T(8,128)S(1)}, f32[2,1,16,128]{3,2,1,0:T(8,128)S(1)}, u32[]{:S(2)}, u32[]{:S(2)}) collective-permute-start(f32[2,1,16,128]{3,2,1,0:T(8,128)S(1)} %add.847), channel_id=1, source_target_pairs={{0,64},{16,80},{32,96},{48,112},{64,0},{80,16},{96,32},{112,48},{1... | collective-permute-start | bytes 49160 | tf_op jit(solution)/shard_map/ppermute | solution.py:81
  325.5 13.7 %collective-permute-start.16 = (f32[2,1,16,128]{3,2,1,0:T(8,128)S(1)}, f32[2,1,16,128]{3,2,1,0:T(8,128)S(1)}, u32[]{:S(2)}, u32[]{:S(2)}) collective-permute-start(f32[2,1,16,128]{3,2,1,0:T(8,128)S(1)} %add.848), channel_id=1, source_target_pairs={{0,128},{16,144},{32,160},{48,176},{64,192},{80,208},{96,224},{112... | collective-permute-start | bytes 49160 | tf_op jit(solution)/shard_map/ppermute | solution.py:81
  333.6 8.1 %collective-permute-start.11 = (f32[18,1,128]{2,0,1:T(8,128)S(1)}, f32[18,1,128]{2,0,1:T(8,128)S(1)}, u32[]{:S(2)}, u32[]{:S(2)}) collective-permute-start(f32[18,1,128]{2,0,1:T(8,128)S(1)} %get-tuple-element.230), channel_id=1, source_target_pairs={{0,16},{16,32},{32,48},{48,64},{64,80},{80,96},{96,112},{112,128},... | collective-permute-start | bytes 27656 | tf_op jit(solution)/shard_map/ppermute | solution.py:21
  335.5 6.1 %collective-permute-start.12 = (f32[18,1,128]{2,0,1:T(8,128)S(1)}, f32[18,1,128]{2,0,1:T(8,128)S(1)}, u32[]{:S(2)}, u32[]{:S(2)}) collective-permute-start(f32[18,1,128]{2,0,1:T(8,128)S(1)} %get-tuple-element.231), channel_id=1, source_target_pairs={{16,0},{32,16},{48,32},{64,48},{80,64},{96,80},{112,96},{128,112},... | collective-permute-start | bytes 27656 | tf_op jit(solution)/shard_map/ppermute | solution.py:23
  339.2 6.0 collective-permute-start.17
  347.1 1.0 copy-start.2
  351.6 11.4 %collective-permute-start.22 = (f32[2,1,16,128]{3,2,1,0:T(8,128)S(1)}, f32[2,1,16,128]{3,2,1,0:T(8,128)S(1)}, u32[]{:S(2)}, u32[]{:S(2)}) collective-permute-start(f32[2,1,16,128]{3,2,1,0:T(8,128)S(1)} %multiply_add_fusion.6), channel_id=1, source_target_pairs={{0,16},{16,0},{32,48},{48,32},{64,80},{80,64},{96,112},{112,96},{1... | collective-permute-start | bytes 49160 | tf_op jit(solution)/shard_map/ppermute | solution.py:81
  357.1 100.0 %collective-permute-start.19 = (f32[1,32,128]{2,0,1:T(1,128)S(1)}, f32[1,32,128]{2,0,1:T(1,128)S(1)}, u32[]{:S(2)}, u32[]{:S(2)}) collective-permute-start(f32[1,32,128]{2,0,1:T(1,128)S(1)} %slice.1124), channel_id=1, source_target_pairs={{1,0},{2,1},{3,2},{4,3},{5,4},{6,5},{7,6},{8,7},{9,8},{10,9},{11,1... | collective-permute-start | bytes 49160 | tf_op jit(solution)/shard_map/ppermute | solution.py:23
  359.0 98.1 %collective-permute-start.18 = (f32[1,32,128]{2,1,0:T(8,128)S(1)}, f32[1,32,128]{2,1,0:T(8,128)S(1)}, u32[]{:S(2)}, u32[]{:S(2)}) collective-permute-start(f32[1,32,128]{2,1,0:T(8,128)S(1)} %slice.1123), channel_id=1, source_target_pairs={{0,1},{1,2},{2,3},{3,4},{4,5},{5,6},{6,7},{7,8},{8,9},{9,10},{10,1... | collective-permute-start | bytes 49160 | tf_op jit(solution)/shard_map/ppermute | solution.py:21
  363.0 5.6 collective-permute-start.23
  368.6 82.9 %collective-permute-start.24 = (f32[2,1,16,128]{3,2,1,0:T(8,128)S(1)}, f32[2,1,16,128]{3,2,1,0:T(8,128)S(1)}, u32[]{:S(2)}, u32[]{:S(2)}) collective-permute-start(f32[2,1,16,128]{3,2,1,0:T(8,128)S(1)} %add.863), channel_id=1, source_target_pairs={{0,64},{16,80},{32,96},{48,112},{64,0},{80,16},{96,32},{112,48},{1... | collective-permute-start | bytes 49160 | tf_op jit(solution)/shard_map/ppermute | solution.py:81
  451.5 11.2 %collective-permute-start.25 = (f32[2,1,16,128]{3,2,1,0:T(8,128)S(1)}, f32[2,1,16,128]{3,2,1,0:T(8,128)S(1)}, u32[]{:S(2)}, u32[]{:S(2)}) collective-permute-start(f32[2,1,16,128]{3,2,1,0:T(8,128)S(1)} %add.864), channel_id=1, source_target_pairs={{0,128},{16,144},{32,160},{48,176},{64,192},{80,208},{96,224},{112... | collective-permute-start | bytes 49160 | tf_op jit(solution)/shard_map/ppermute | solution.py:81
  457.1 8.1 %collective-permute-start.20 = (f32[18,1,128]{2,0,1:T(8,128)S(1)}, f32[18,1,128]{2,0,1:T(8,128)S(1)}, u32[]{:S(2)}, u32[]{:S(2)}) collective-permute-start(f32[18,1,128]{2,0,1:T(8,128)S(1)} %get-tuple-element.228), channel_id=1, source_target_pairs={{0,16},{16,32},{32,48},{48,64},{64,80},{80,96},{96,112},{112,128},... | collective-permute-start | bytes 27656 | tf_op jit(solution)/shard_map/ppermute | solution.py:21
  459.1 6.1 %collective-permute-start.21 = (f32[18,1,128]{2,0,1:T(8,128)S(1)}, f32[18,1,128]{2,0,1:T(8,128)S(1)}, u32[]{:S(2)}, u32[]{:S(2)}) collective-permute-start(f32[18,1,128]{2,0,1:T(8,128)S(1)} %get-tuple-element.229), channel_id=1, source_target_pairs={{16,0},{32,16},{48,32},{64,48},{80,64},{96,80},{112,96},{128,112},... | collective-permute-start | bytes 27656 | tf_op jit(solution)/shard_map/ppermute | solution.py:23
  462.7 6.0 collective-permute-start.26
  470.6 1.0 copy-start.3
  475.1 11.4 %collective-permute-start.31 = (f32[2,1,16,128]{3,2,1,0:T(8,128)S(1)}, f32[2,1,16,128]{3,2,1,0:T(8,128)S(1)}, u32[]{:S(2)}, u32[]{:S(2)}) collective-permute-start(f32[2,1,16,128]{3,2,1,0:T(8,128)S(1)} %multiply_add_fusion.5), channel_id=1, source_target_pairs={{0,16},{16,0},{32,48},{48,32},{64,80},{80,64},{96,112},{112,96},{1... | collective-permute-start | bytes 49160 | tf_op jit(solution)/shard_map/ppermute | solution.py:81
  480.6 103.3 %collective-permute-start.28 = (f32[1,32,128]{2,0,1:T(1,128)S(1)}, f32[1,32,128]{2,0,1:T(1,128)S(1)}, u32[]{:S(2)}, u32[]{:S(2)}) collective-permute-start(f32[1,32,128]{2,0,1:T(1,128)S(1)} %slice.1140), channel_id=1, source_target_pairs={{1,0},{2,1},{3,2},{4,3},{5,4},{6,5},{7,6},{8,7},{9,8},{10,9},{11,1... | collective-permute-start | bytes 49160 | tf_op jit(solution)/shard_map/ppermute | solution.py:23
  482.5 101.4 %collective-permute-start.27 = (f32[1,32,128]{2,1,0:T(8,128)S(1)}, f32[1,32,128]{2,1,0:T(8,128)S(1)}, u32[]{:S(2)}, u32[]{:S(2)}) collective-permute-start(f32[1,32,128]{2,1,0:T(8,128)S(1)} %slice.1139), channel_id=1, source_target_pairs={{0,1},{1,2},{2,3},{3,4},{4,5},{5,6},{6,7},{7,8},{8,9},{9,10},{10,1... | collective-permute-start | bytes 49160 | tf_op jit(solution)/shard_map/ppermute | solution.py:21
  486.5 5.6 collective-permute-start.32
  492.1 84.7 %collective-permute-start.33 = (f32[2,1,16,128]{3,2,1,0:T(8,128)S(1)}, f32[2,1,16,128]{3,2,1,0:T(8,128)S(1)}, u32[]{:S(2)}, u32[]{:S(2)}) collective-permute-start(f32[2,1,16,128]{3,2,1,0:T(8,128)S(1)} %add.879), channel_id=1, source_target_pairs={{0,64},{16,80},{32,96},{48,112},{64,0},{80,16},{96,32},{112,48},{1... | collective-permute-start | bytes 49160 | tf_op jit(solution)/shard_map/ppermute | solution.py:81
  576.8 12.7 %collective-permute-start.34 = (f32[2,1,16,128]{3,2,1,0:T(8,128)S(1)}, f32[2,1,16,128]{3,2,1,0:T(8,128)S(1)}, u32[]{:S(2)}, u32[]{:S(2)}) collective-permute-start(f32[2,1,16,128]{3,2,1,0:T(8,128)S(1)} %add.880), channel_id=1, source_target_pairs={{0,128},{16,144},{32,160},{48,176},{64,192},{80,208},{96,224},{112... | collective-permute-start | bytes 49160 | tf_op jit(solution)/shard_map/ppermute | solution.py:81
  584.0 8.1 %collective-permute-start.29 = (f32[18,1,128]{2,0,1:T(8,128)S(1)}, f32[18,1,128]{2,0,1:T(8,128)S(1)}, u32[]{:S(2)}, u32[]{:S(2)}) collective-permute-start(f32[18,1,128]{2,0,1:T(8,128)S(1)} %get-tuple-element.226), channel_id=1, source_target_pairs={{0,16},{16,32},{32,48},{48,64},{64,80},{80,96},{96,112},{112,128},... | collective-permute-start | bytes 27656 | tf_op jit(solution)/shard_map/ppermute | solution.py:21
  585.9 6.1 %collective-permute-start.30 = (f32[18,1,128]{2,0,1:T(8,128)S(1)}, f32[18,1,128]{2,0,1:T(8,128)S(1)}, u32[]{:S(2)}, u32[]{:S(2)}) collective-permute-start(f32[18,1,128]{2,0,1:T(8,128)S(1)} %get-tuple-element.227), channel_id=1, source_target_pairs={{16,0},{32,16},{48,32},{64,48},{80,64},{96,80},{112,96},{128,112},... | collective-permute-start | bytes 27656 | tf_op jit(solution)/shard_map/ppermute | solution.py:23
  589.6 6.0 collective-permute-start.35
Sparse Core Ops, SparseCore 0:
  32.3 170.0 all-reduce.11
